TPU v7x, 256 devices: a whole 4x4x8 slice. The times are simulated.
256 devices in a mesh: tm: 64 (over z_lo, x, y, core), tensor: 4 (over z_hi).
Axes of the slice: x: 4, y: 4, z: 8 (z_hi: 4, z_lo: 2; z = z_hi * 2 + z_lo), core: 2. Of those that a mesh axis runs over, the one named last changes fastest.
Arguments:
- inputs: bfloat16 [131072, 1536], P('tm', 'tensor'), may hold values from -6 to 6
- kernel: bfloat16 [131072, 1536], P('tm', 'tensor'), may hold values from -5 to 5
- w_in: bfloat16 [12, 128, 128], P('tensor'), may hold values from -0.5 to 0.5
- w_gate: bfloat16 [12, 128, 128], P('tensor'), may hold values from -0.5 to 0.5
- w_out: bfloat16 [12, 128, 128], P('tensor'), may hold values from -0.5 to 0.5
- factor_a: bfloat16 [512, 512], replicated, may hold values from -0.25 to 0.25
- factor_b: bfloat16 [256, 256], replicated, may hold values from -0.375 to 0.375
- cotangent: bfloat16 [131072, 1536], P('tm', 'tensor'), may hold values from -6 to 6
Outputs:
- outputs: bfloat16 [131072, 1536], P('tm', 'tensor')
- grad_inputs: bfloat16 [131072, 1536], P('tm', 'tensor')
- grad_kernel: bfloat16 [131072, 1536], P('tm', 'tensor')
- grad_w_in: float32 [12, 128, 128], P('tensor')
- grad_w_gate: float32 [12, 128, 128], P('tensor')
- grad_w_out: float32 [12, 128, 128], P('tensor')
- grad_factor_a: float32 [512, 512], P('tm')
- grad_factor_b: float32 [256, 256], P('tm')
All inputs are finite; a program needn't handle non-finite values.
Results may differ from a plain program's by a relative error of at most 0.0071.
Values may be sent and summed in bfloat16 or wider, within the bound.
A program may use at most 128 MiB of HBM per device.

v0:
```python
import math

import jax
import jax.numpy as jnp
from jax import lax
from jax.sharding import PartitionSpec as P

D = 1536
N1 = 256
N2 = 512


def mix(act, weight):
    width = weight.shape[1]
    blocks = act.reshape(act.shape[0], weight.shape[0], width)
    out = jnp.einsum("tnb,nbe->tne", blocks, weight, preferred_element_type=jnp.float32)
    return out.reshape(act.shape[0], act.shape[1])


def mix_back(grad, weight):
    width = weight.shape[1]
    blocks = grad.reshape(grad.shape[0], weight.shape[0], width)
    out = jnp.einsum("tne,nbe->tnb", blocks, weight, preferred_element_type=jnp.float32)
    return out.reshape(grad.shape[0], grad.shape[1])


def mix_grad(act, grad, weight):
    width = weight.shape[1]
    left = act.reshape(act.shape[0], weight.shape[0], width)
    right = grad.reshape(grad.shape[0], weight.shape[0], width)
    return jnp.einsum("tnb,tne->nbe", left, right, preferred_element_type=jnp.float32)


def to_columns(values):
    return lax.all_to_all(values, "tm", split_axis=1, concat_axis=0, tiled=True)


def to_rows(values):
    return lax.all_to_all(values, "tm", split_axis=0, concat_axis=1, tiled=True)


def body(inputs, kernel, w_in, w_gate, w_out, factor_a, factor_b, cotangent):
    rows, chans = inputs.shape
    inner = factor_a.shape[0]
    local = rows // inner
    mixed_in = mix(inputs, w_in).astype(jnp.bfloat16)
    gate = mix(inputs, w_gate)
    mixed3 = mixed_in.reshape(local, inner, chans)
    first = jnp.einsum("ijc,jk->ikc", mixed3, factor_a, preferred_element_type=jnp.float32)
    twiddle = kernel.reshape(local, inner, chans).astype(jnp.float32)
    twisted = (first * twiddle).astype(jnp.bfloat16)
    twisted_cols = to_columns(twisted)
    second_cols = jnp.einsum(
        "im,ikc->mkc", factor_b, twisted_cols, preferred_element_type=jnp.float32
    )
    second_rows = to_rows(second_cols.astype(jnp.bfloat16))
    second = second_rows.reshape(rows, chans)
    second32 = second.astype(jnp.float32)
    gated = (second32 * gate).astype(jnp.bfloat16)
    outputs = mix(gated, w_out).astype(jnp.bfloat16)
    grad_gated = mix_back(cotangent, w_out)
    grad_second = (grad_gated * gate).astype(jnp.bfloat16)
    grad_gate = (grad_gated * second32).astype(jnp.bfloat16)
    grad_second_cols = to_columns(grad_second.reshape(local, inner, chans))
    grad_twisted_cols = jnp.einsum(
        "im,mkc->ikc", factor_b, grad_second_cols, preferred_element_type=jnp.float32
    )
    factor_b_part = jnp.einsum(
        "ikc,mkc->im", twisted_cols, grad_second_cols, preferred_element_type=jnp.float32
    )
    grad_twisted = to_rows(grad_twisted_cols.astype(jnp.bfloat16))
    grad_tw32 = grad_twisted.astype(jnp.float32)
    grad_first = (grad_tw32 * twiddle).astype(jnp.bfloat16)
    grad_kernel = (grad_tw32 * first).astype(jnp.bfloat16).reshape(rows, chans)
    factor_a_part = jnp.einsum(
        "ijc,ikc->jk", mixed3, grad_first, preferred_element_type=jnp.float32
    )
    grad_mixed = jnp.einsum("jk,ikc->ijc", factor_a, grad_first, preferred_element_type=jnp.float32)
    grad_mixed = grad_mixed.astype(jnp.bfloat16).reshape(rows, chans)
    grad_inputs = (mix_back(grad_mixed, w_in) + mix_back(grad_gate, w_gate)).astype(jnp.bfloat16)
    mixer_terms = (
        mix_grad(inputs, grad_mixed, w_in),
        mix_grad(inputs, grad_gate, w_gate),
        mix_grad(gated, cotangent, w_out),
    )
    summed_in, summed_gate, summed_out = lax.psum(
        (mixer_terms[0], mixer_terms[1], mixer_terms[2]), "tm"
    )
    token_scale = 1.0 / math.sqrt(N1 * N2)
    factor_terms = (factor_a_part, factor_b_part)
    factor_terms = lax.psum((factor_terms[0], factor_terms[1]), "tensor")
    factor_pieces = (
        lax.psum_scatter(factor_terms[0], "tm", scatter_dimension=0, tiled=True),
        lax.psum_scatter(factor_terms[1], "tm", scatter_dimension=0, tiled=True),
    )
    grad_factor_a = factor_pieces[0] / math.sqrt(N1 * D)
    grad_factor_b = factor_pieces[1] / math.sqrt(N2 * D)
    return (
        outputs,
        grad_inputs,
        grad_kernel,
        summed_in * token_scale,
        summed_gate * token_scale,
        summed_out * token_scale,
        grad_factor_a,
        grad_factor_b,
    )


def solution(mesh):
    return jax.shard_map(
        body,
        mesh=mesh,
        in_specs=(
            P("tm", "tensor"),
            P("tm", "tensor"),
            P("tensor", None, None),
            P("tensor", None, None),
            P("tensor", None, None),
            P(),
            P(),
            P("tm", "tensor"),
        ),
        out_specs=(
            P("tm", "tensor"),
            P("tm", "tensor"),
            P("tm", "tensor"),
            P("tensor", None, None),
            P("tensor", None, None),
            P("tensor", None, None),
            P("tm", None),
            P("tm", None),
        ),
        check_vma=False,
    )
```

profile of v0, /device:TPU:1, one launch (start us, length us, event | category | flops | bytes accessed | tf_op | source)
XLA Modules:
  0.0 1054.2 jit_solution(8851953927329009670)
XLA Ops:
  7.2 1.8 copy.84
  9.0 2.6 copy.100
  13.0 2.7 fusion
  15.8 3.8 convert_element_type.119
  19.6 4.1 copy.102
  23.7 32.8 %all_to_all.54 = bf16[4,512,384]{2,0,1:T(4,128)(2,1)S(1)} all-to-all(bf16[4,512,384]{2,0,1:T(4,128)(2,1)} %copy.102), channel_id=1, replica_groups=mesh['tm'=64,'tensor'=4] {'tm'}, dimensions={1} | all-to-all | bytes 3145728 | tf_op jit(solution)/shard_map/all_to_all | solution.py:35
  56.9 1.1 copy-done.10
  58.1 1.8 fusion.7
  59.8 2.9 copy.106
  62.8 6.6 all-to-all-start.3
  69.3 1.8 fusion.5
  71.1 3.9 convert_element_type.104
  75.0 3.9 copy.119
  78.8 3.0 copy.88
  81.9 9.9 all-to-all-done.3
  91.7 3.2 copy_bitcast_fusion
  95.0 3.6 copy.113
  98.6 6.0 fusion.4
  104.6 3.8 copy.89
  108.4 28.7 %all_to_all.55 = bf16[4,512,384]{2,0,1:T(4,128)(2,1)S(1)} all-to-all(bf16[4,512,384]{2,0,1:T(4,128)(2,1)} %copy.89), channel_id=1, replica_groups=mesh['tm'=64,'tensor'=4] {'tm'}, dimensions={1} | all-to-all | bytes 3145728 | tf_op jit(solution)/shard_map/all_to_all | solution.py:35
  137.5 1.1 copy-done.13
  138.6 1.8 fusion.6
  140.5 2.9 copy.93
  143.4 6.6 all-to-all-start.1
  150.1 2.9 fusion.8
  153.0 2.4 copy.109
  155.4 3.8 reshape_reshape.4
  159.2 2.8 convolution_bitcast_fusion.2
  162.0 1.3 fusion.14
  163.4 9.0 all-to-all-done.1
  172.4 1.8 convert_bitcast_fusion.1
  174.2 2.0 copy.94
  176.2 5.7 reshape.69
  181.9 4.9 copy.97
  186.8 4.9 fusion.1
  191.8 1.4 convolution_bitcast_fusion.1
  193.5 0.9 copy-done.4
  194.4 1.3 fusion.25
  195.8 3.9 convolution_bitcast_fusion
  201.0 2.7 copy.114
  205.1 1.7 add_convert_fusion
  206.8 2.7 copy.123
  209.5 1.8 convolution_convert_fusion
  211.3 2.6 copy.122
  213.9 523.0 %all-reduce.5.cloned.1.call-done = (f32[3,128,128]{1,2,0:T(8,128)}, f32[3,128,128]{1,2,0:T(8,128)}, f32[3,128,128]{1,2,0:T(8,128)}, f32[256,256]{1,0:T(8,128)}) async-done(((f32[3,128,128]{1,2,0:T(8,128)}, f32[3,128,128]{1,2,0:T(8,128)}, f32[3,128,128]{1,2,0:T(8,128)}, f32[256,256]{1,0:T(8,128)}), (f32[3,128,128]{1,2,0:T(8,128)}, f32[3,128,128]{1,2,0:T(8,128)}, f32[3,128,128]{1,2,0:T(8,128)}, ...) | async-done | bytes 851984 | tf_op jit(solution)/shard_map/psum | solution.py:86
  737.6 288.8 %reduce-scatter.2.cloned.1.call-done = f32[8,512]{1,0:T(8,128)} async-done(((f32[512,512]{1,0:T(8,128)}), f32[8,512]{1,0:T(8,128)}) %reduce-scatter.2.cloned.1.call-update) | async-done | bytes 16400 | tf_op jit(solution)/shard_map/reduce_scatter | solution.py:93
  1026.4 16.2 %all-reduce.2 = (f32[8,512]{1,0:T(8,128)S(1)}, f32[4,256]{1,0:T(4,128)S(1)}) all-reduce(f32[8,512]{1,0:T(8,128)} %reduce-scatter.2.cloned.1.call-done, f32[4,256]{1,0:T(4,128)S(1)} %constant_dynamic-slice_fusion), channel_id=1, replica_groups=mesh['tm'=64,'tensor'=4] {'tensor'}, use_global_device_ids=true, to_apply=%region_3.0 | all-reduce | flops 5120 | bytes 40960 | tf_op jit(solution)/shard_map/psum | solution.py:91
  1043.8 1.1 broadcast_multiply_fusion
  (57 shorter events, 9.0 us)
Async XLA Ops:
  7.2 91.4 %copy-start = (bf16[512,512]{1,0:T(8,128)(2,1)S(1)}, bf16[512,512]{1,0:T(8,128)(2,1)}, u32[]{:S(2)}) copy-start(bf16[512,512]{1,0:T(8,128)(2,1)} %param.13) | copy-start | bytes 1572868
  9.0 2.6 copy-start.17
  11.6 1.4 copy-start.3
  11.6 1.4 copy-start.15
  12.2 3.5 copy-start.2
  56.7 1.3 copy-start.19
  56.9 1.2 copy-start.10
  62.7 6.6 copy-start.16
  62.8 29.0 %all-to-all-start.3 = ((bf16[256,8,384]{2,1,0:T(8,128)(2,1)}), bf16[256,8,384]{2,1,0:T(8,128)(2,1)}, u32[]{:S(2)}, u32[]{:S(2)}) async-start(bf16[256,8,384]{2,1,0:T(8,128)(2,1)} %copy.106), calls=%async_computation.3 | async-start | bytes 3145728 | tf_op jit(solution)/shard_map/all_to_all | solution.py:39
  137.5 1.1 copy-start.13
  143.4 29.0 %all-to-all-start.1 = ((bf16[256,8,384]{2,1,0:T(8,128)(2,1)}), bf16[256,8,384]{2,1,0:T(8,128)(2,1)}, u32[]{:S(2)}, u32[]{:S(2)}) async-start(bf16[256,8,384]{2,1,0:T(8,128)(2,1)} %copy.93), calls=%async_computation.1 | async-start | bytes 3145728 | tf_op jit(solution)/shard_map/all_to_all | solution.py:39
  150.0 586.9 %all-reduce.5.cloned.1.call-start = ((), (), s32[]{:S(2)}) async-start(), calls=%async_computation.6 | async-start | bytes 1703936 | tf_op jit(solution)/shard_map/psum | solution.py:86
  159.2 2.8 copy-start.11
  159.2 2.8 copy-start.14
  191.8 1.5 copy-start.8
  191.8 1.7 copy-start.5
  191.8 2.6 copy-start.4
  194.4 1.4 copy-start.12
  195.7 4.0 copy-start.20
  195.7 830.8 %reduce-scatter.2.cloned.1.call-start = ((), (), s32[]{:S(2)}) async-start(), calls=%async_computation.5 | async-start | bytes 1064960 | tf_op jit(solution)/shard_map/reduce_scatter | solution.py:93
  201.0 2.7 copy-start.7
  203.7 1.4 copy-start.9
  206.8 2.7 copy-start.6
  211.3 836.1 %copy-start.1 = (bf16[512,512]{1,0:T(8,128)(2,1)S(1)}, bf16[512,512]{1,0:T(8,128)(2,1)}, u32[]{:S(2)}) copy-start(bf16[512,512]{1,0:T(8,128)(2,1)} %param.13) | copy-start | bytes 1572868
  736.9 309.6 %copy-start.18 = (f32[3,128,128]{1,2,0:T(8,128)S(1)}, f32[3,128,128]{1,2,0:T(8,128)}, u32[]{:S(2)}) copy-start(f32[3,128,128]{1,2,0:T(8,128)} %get-tuple-element.32) | copy-start | bytes 589828
Sparse Core Ops, SparseCore 0:
  195.8 541.0 all-reduce.4
  739.4 286.9 reduce-scatter.1
where the time goes:
time: 1060 us; the launch traced here: 1050 us
  waiting for transfers between devices  831 us (78%)
  blocking collectives  77.7 us (7%)
  local copies, waits for them, and re-layouts  72.9 us (7%)
  matrix products  32.4 us (3%)
  between operations  14.9 us (1%)
  starting transfers between devices  13.3 us (1%)
  other arithmetic  12.3 us (1%)
    psum x1, waiting for transfers between devices, body(): lax.psum((mixer_terms[0], mixer_terms[1], mixer_terms[2]), 'tm')  523 us
    reduce_scatter x1, waiting for transfers between devices, body(): lax.psum_scatter(factor_terms[0], 'tm', scatter_dimension=0, tiled=True)  289 us
    all_to_all x2, blocking collectives, to_columns(): return lax.all_to_all(values, 'tm', split_axis=1, concat_axis=0, tiled=True)  61.5 us
  transfers between devices with their start and end apart: 4, of which 4 were waited for; matrix products, arithmetic and copies ran while one was open for 4% of the time, Pallas kernels for 0%

commit v1 on v0

v1 whole, which is shorter than its diff:
```python
import math

import jax
import jax.numpy as jnp
from jax import lax
from jax.experimental import pallas as pl
from jax.experimental.pallas import tpu as pltpu
from jax.sharding import PartitionSpec as P

D = 1536
N1 = 256
N2 = 512
MESH = pl.DeviceIdType.MESH
F32 = jnp.float32
BF16 = jnp.bfloat16
TM = 64
TE = 4
ROWS = 2048
CH = 384
LOC = 4
KD = 8
NB = 3
DC = 8
CR = DC * KD


def lanes(n):
    return slice(n * 128, (n + 1) * 128)


def nt(a, b):
    return lax.dot_general(a, b, (((1,), (1,)), ((), ())), preferred_element_type=F32)


def nn(a, b):
    return jnp.dot(a, b, preferred_element_type=F32)


def four(ref, c, n):
    return jnp.concatenate(
        [ref[pl.ds(i * N2 + c * CR, CR), lanes(n)] for i in range(LOC)], axis=0
    )


def put_four(ref, c, n, val):
    for i in range(LOC):
        ref[pl.ds(i * N2 + c * CR, CR), lanes(n)] = val[i * CR : (i + 1) * CR]


def by_dest(val):
    return jnp.concatenate(
        [
            val[i * CR + d * KD : i * CR + (d + 1) * KD]
            for d in range(DC)
            for i in range(LOC)
        ],
        axis=0,
    )


def by_block(val):
    return jnp.concatenate(
        [
            val[(d * LOC + i) * KD : (d * LOC + i + 1) * KD]
            for i in range(LOC)
            for d in range(DC)
        ],
        axis=0,
    )


def kernel_body(
    in_h,
    ker_h,
    w_in,
    w_gate,
    w_out,
    fa,
    fb,
    cot_h,
    out_h,
    gin_h,
    gker_h,
    gw_in,
    gw_gate,
    gw_out,
    gfa,
    gfb,
    in_v,
    ker_v,
    cot_v,
    in_t,
    cot_t,
    a_t,
    b_t,
    gate_v,
    gg_v,
    first_v,
    mx_v,
    so_g,
    so_f,
    rc_g,
    rc_f,
    xs,
    x_g,
    x_f,
    sr_g,
    sr_f,
    rr_g,
    rr_f,
    gf_v,
    gm_v,
    gated_v,
    ggate_v,
    out_v,
    gin_v,
    gker_v,
    fb_acc,
    fa_acc,
    r1s,
    r1r,
    r2s,
    r2r,
    tr,
    pr,
    ag1,
    ag2,
    ld_sem,
    st_sem,
    snd,
    rcv,
):
    me = lax.axis_index("tm")
    te = lax.axis_index("tensor")
    core = lax.rem(me, 2)
    my = lax.rem(me // 2, 4)
    mx = lax.rem(me // 8, 4)
    mz = me // 32

    def peer(p):
        o = lax.rem((p - 1) * 37, 63) + 1
        dc = lax.rem(core + lax.rem(o, 2), 2)
        dy = lax.rem(my + lax.rem(o // 2, 4), 4)
        dx = lax.rem(mx + lax.rem(o // 8, 4), 4)
        dz = lax.rem(mz + o // 32, 2)
        return ((dz * 4 + dx) * 4 + dy) * 2 + dc

    loads = [
        pltpu.make_async_copy(cot_h, cot_v, ld_sem.at[0]),
        pltpu.make_async_copy(in_h, in_v, ld_sem.at[1]),
        pltpu.make_async_copy(ker_h, ker_v, ld_sem.at[2]),
    ]
    for cp in loads:
        cp.start()

    barrier = pltpu.get_barrier_semaphore()

    @pl.loop(1, TM)
    def _(p):
        pl.semaphore_signal(barrier, inc=1, device_id=(peer(p), te), device_id_type=MESH)

    for q in range(1, TE):
        pl.semaphore_signal(
            barrier, inc=1, device_id=(me, lax.rem(te + q, TE)), device_id_type=MESH
        )

    def copy_to(src, dst, ph, device):
        return pltpu.make_async_remote_copy(
            src_ref=src,
            dst_ref=dst,
            send_sem=snd.at[ph],
            recv_sem=rcv.at[ph],
            device_id=device,
            device_id_type=MESH,
        )

    def send_all(slot_of, dst, ph):
        @pl.loop(1, TM)
        def _(p):
            d = peer(p)
            copy_to(slot_of(d), dst.at[me], ph, (d, te)).start()

    def wait_slots(ref, sem, slots=TM - 1):
        part = ref.at[pl.ds(0, slots)]
        pltpu.make_async_copy(part, part, sem).wait()

    loads[0].wait()
    loads[1].wait()

    @pl.loop(0, N2 // CR)
    def _(c):
        for n in range(NB):
            gate = nn(four(in_v, c, n), w_gate[n])
            gg = nt(four(cot_v, c, n), w_out[n])
            put_four(gate_v, c, n, gate)
            put_four(gg_v, c, n, gg)
            so_g[pl.ds(c * DC, DC), :, lanes(n)] = (
                by_dest(gate * gg).astype(BF16).reshape(DC, LOC * KD, 128)
            )

    pl.semaphore_wait(barrier, TM - 1 + TE - 1)
    send_all(lambda d: so_g.at[d], rc_g, 0)

    for s in range(4):
        a_t[:, lanes(s)] = fa[lanes(s), :].T

    @pl.loop(0, LOC)
    def _(i):
        rows = pl.ds(pl.multiple_of(i * N2, N2), N2)
        for n in range(NB):
            mx_v[rows, lanes(n)] = nn(in_v[rows, lanes(n)], w_in[n]).astype(BF16)
        first_v[rows, :] = nn(a_t[...], mx_v[rows, :])

    loads[2].wait()

    @pl.loop(0, N2 // CR)
    def _(c):
        for n in range(NB):
            tw = four(first_v, c, n) * four(ker_v, c, n).astype(F32)
            so_f[pl.ds(c * DC, DC), :, lanes(n)] = (
                by_dest(tw).astype(BF16).reshape(DC, LOC * KD, 128)
            )

    send_all(lambda d: so_f.at[d], rc_f, 1)
    rc_g[me] = so_g[me]
    rc_f[me] = so_f[me]

    b_t[...] = fb[...].T

    @pl.loop(0, ROWS // 256)
    def _(c):
        rows = pl.ds(pl.multiple_of(c * 256, 256), 256)
        for n in range(NB):
            in_t[n, :, rows] = in_v[rows, lanes(n)].T
            cot_t[n, :, rows] = cot_v[rows, lanes(n)].T

    def columns(rc, x):
        @pl.loop(0, 8)
        def _(c):
            rows = pl.ds(pl.multiple_of(c * 256, 256), 256)
            for n in range(NB):
                xs[n, rows, :] = rc[pl.ds(c * 8, 8), :, lanes(n)].reshape(256, 128).astype(F32)

        for k in range(KD):
            for n in range(NB):
                x[k, :, lanes(n)] = xs[n, pl.ds(k, N1, stride=KD), :].astype(BF16)

    def product(lhs, x, sr):
        for k in range(KD):
            y = nn(lhs[...], x[k])
            for n in range(NB):
                xs[n, pl.ds(k, N1, stride=KD), :] = y[:, lanes(n)]

        @pl.loop(0, 8)
        def _(c):
            rows = pl.ds(pl.multiple_of(c * 256, 256), 256)
            for n in range(NB):
                sr[pl.ds(c * 8, 8), :, lanes(n)] = (
                    xs[n, rows, :].astype(BF16).reshape(8, LOC * KD, 128)
                )

    wait_slots(rc_g, rcv.at[0])
    columns(rc_g, x_g)
    product(fb, x_g, sr_g)
    send_all(lambda d: sr_g.at[d], rr_g, 2)
    rr_g[me] = sr_g[me]

    wait_slots(rc_f, rcv.at[1])
    columns(rc_f, x_f)
    product(b_t, x_f, sr_f)
    send_all(lambda d: sr_f.at[d], rr_f, 3)
    rr_f[me] = sr_f[me]

    fb_acc[...] = nt(x_f[0], x_g[0])

    @pl.loop(1, KD)
    def _(k):
        fb_acc[...] += nt(x_f[k], x_g[k])

    for h in range(2):
        r1s[:, h, :, 512:640] = fb_acc[:, lanes(h)].reshape(TM // 2, 8, 128)

    wait_slots(rr_g, rcv.at[2])

    @pl.loop(0, N2 // CR)
    def _(c):
        for n in range(NB):
            gt = by_block(
                rr_g[pl.ds(c * DC, DC), :, lanes(n)].reshape(LOC * CR, 128).astype(F32)
            )
            gf = (gt * four(ker_v, c, n).astype(F32)).astype(BF16)
            gk = (gt * four(first_v, c, n)).astype(BF16)
            put_four(gf_v, c, n, gf)
            put_four(gker_v, c, n, gk)

    stores = [
        pltpu.make_async_copy(gker_v, gker_h, st_sem.at[0]),
        pltpu.make_async_copy(out_v, out_h, st_sem.at[1]),
        pltpu.make_async_copy(gin_v, gin_h, st_sem.at[2]),
    ]
    stores[0].start()

    fa_acc[...] = jnp.zeros_like(fa_acc)

    @pl.loop(0, LOC)
    def _(i):
        rows = pl.ds(pl.multiple_of(i * N2, N2), N2)
        gm_v[rows, :] = nn(fa[...], gf_v[rows, :]).astype(BF16)
        fa_acc[...] += nt(mx_v[rows, :], gf_v[rows, :])

    r1s[:, :, :, 0:512] = fa_acc[...].reshape(TM // 2, 2, 8, 512)
    for n in range(NB):
        r1s[n * 8 : (n + 1) * 8, :, :, 640:768] = nn(in_t[n], gm_v[:, lanes(n)]).reshape(
            8, 2, 8, 128
        )
    r1s[24:32, :, :, 640:768] = jnp.zeros((8, 2, 8, 128), F32)
    send_all(lambda d: r1s.at[d // 2, lax.rem(d, 2)], r1r, 4)
    r1r[me] = r1s[me // 2, core]

    wait_slots(rr_f, rcv.at[3])

    @pl.loop(0, N2 // CR)
    def _(c):
        for n in range(NB):
            sec = by_block(
                rr_f[pl.ds(c * DC, DC), :, lanes(n)].reshape(LOC * CR, 128).astype(F32)
            )
            put_four(gated_v, c, n, (sec * four(gate_v, c, n)).astype(BF16))
            put_four(ggate_v, c, n, (sec * four(gg_v, c, n)).astype(BF16))

    for n in range(NB):
        r2s[n * 16 : (n + 1) * 16, 0] = nn(in_t[n], ggate_v[:, lanes(n)]).reshape(16, 8, 128)
        r2s[n * 16 : (n + 1) * 16, 1] = nn(cot_t[n], gated_v[:, lanes(n)]).T.reshape(16, 8, 128)
    r2s[48:64] = jnp.zeros((16, 2, 8, 128), F32)
    send_all(lambda d: r2s.at[d], r2r, 7)
    r2r[me] = r2s[me]

    @pl.loop(0, ROWS // 256)
    def _(c):
        rows = pl.ds(pl.multiple_of(c * 256, 256), 256)
        for n in range(NB):
            out_v[rows, lanes(n)] = nn(gated_v[rows, lanes(n)], w_out[n]).astype(BF16)
            gin_v[rows, lanes(n)] = (
                nt(gm_v[rows, lanes(n)], w_in[n]) + nt(ggate_v[rows, lanes(n)], w_gate[n])
            ).astype(BF16)

    stores[1].start()
    stores[2].start()

    token_scale = 1.0 / math.sqrt(N1 * N2)
    wait_slots(r1r, rcv.at[4])
    sum1 = lax.fori_loop(1, TM, lambda q, acc: acc + r1r[q], r1r[0])
    tr[te] = sum1[:, 0:640]
    for q in range(1, TE):
        copy_to(tr.at[te], tr.at[te], 5, (me, lax.rem(te + q, TE))).start()
    ag1[me] = sum1[:, 640:768] * token_scale
    send_all(lambda d: ag1.at[me], ag1, 8)

    wait_slots(r2r, rcv.at[7])
    sum2 = lax.fori_loop(1, TM, lambda q, acc: acc + r2r[q], r2r[0])
    ag2[me] = sum2 * token_scale
    send_all(lambda d: ag2.at[me], ag2, 9)

    wait_slots(tr, rcv.at[5], TE - 1)
    total = tr[0] + tr[1] + tr[2] + tr[3]
    gfa[...] = total[:, 0:512] * (1.0 / math.sqrt(N1 * D))
    pr[core] = total[:, 512:640] * (1.0 / math.sqrt(N2 * D))
    pair = copy_to(pr.at[core], pr.at[core], 6, (me + 1 - 2 * core, te))
    pair.start()
    pair.wait()
    for h in range(2):
        gfb[:, lanes(h)] = jnp.where(core == 0, pr[h, 0:4, :], pr[h, 4:8, :])

    wait_slots(ag1, rcv.at[8])
    gw_in[...] = ag1[0:48]
    wait_slots(ag2, rcv.at[9])
    gw_gate[...] = ag2[0:48, 0]
    gw_out[...] = ag2[0:48, 1]

    wait_slots(rc_g, snd.at[0])
    wait_slots(rc_f, snd.at[1])
    wait_slots(rr_g, snd.at[2])
    wait_slots(rr_f, snd.at[3])
    wait_slots(r1r, snd.at[4])
    wait_slots(tr, snd.at[5], TE - 1)
    wait_slots(r2r, snd.at[7])
    wait_slots(ag1, snd.at[8])
    wait_slots(ag2, snd.at[9])
    for cp in stores:
        cp.wait()


def body(inputs, kernel, w_in, w_gate, w_out, factor_a, factor_b, cotangent):
    any_spec = pl.BlockSpec(memory_space=pl.ANY)
    vm = pl.BlockSpec(memory_space=pltpu.VMEM)
    big = jax.ShapeDtypeStruct((ROWS, CH), BF16)
    wide = pltpu.VMEM((ROWS, CH), F32)
    act = pltpu.VMEM((ROWS, CH), BF16)
    turned = pltpu.VMEM((NB, 128, ROWS), BF16)
    slots = pltpu.VMEM((TM, LOC * KD, CH), BF16)
    cols = pltpu.VMEM((KD, N1, CH), BF16)
    tile = jax.ShapeDtypeStruct((48, 8, 128), F32)
    outs = pl.pallas_call(
        kernel_body,
        name="monarch",
        out_shape=(
            big,
            big,
            big,
            tile,
            tile,
            tile,
            jax.ShapeDtypeStruct((8, N2), F32),
            jax.ShapeDtypeStruct((4, N1), F32),
        ),
        in_specs=[any_spec, any_spec, vm, vm, vm, vm, vm, any_spec],
        out_specs=(any_spec, any_spec, any_spec, vm, vm, vm, vm, vm),
        scratch_shapes=[
            act,
            act,
            act,
            turned,
            turned,
            pltpu.VMEM((N2, N2), BF16),
            pltpu.VMEM((N1, N1), BF16),
            wide,
            wide,
            wide,
            act,
            slots,
            slots,
            slots,
            slots,
            pltpu.VMEM((NB, ROWS, 128), F32),
            cols,
            cols,
            slots,
            slots,
            slots,
            slots,
            act,
            act,
            act,
            act,
            act,
            act,
            act,
            pltpu.VMEM((N1, N1), F32),
            pltpu.VMEM((N2, N2), F32),
            pltpu.VMEM((TM // 2, 2, 8, 768), F32),
            pltpu.VMEM((TM, 8, 768), F32),
            pltpu.VMEM((TM, 2, 8, 128), F32),
            pltpu.VMEM((TM, 2, 8, 128), F32),
            pltpu.VMEM((TE, 8, 640), F32),
            pltpu.VMEM((2, 8, 128), F32),
            pltpu.VMEM((TM, 8, 128), F32),
            pltpu.VMEM((TM, 2, 8, 128), F32),
            pltpu.SemaphoreType.DMA((3,)),
            pltpu.SemaphoreType.DMA((3,)),
            pltpu.SemaphoreType.DMA((10,)),
            pltpu.SemaphoreType.DMA((10,)),
        ],
        compiler_params=pltpu.CompilerParams(
            collective_id=0, has_side_effects=True, vmem_limit_bytes=67043328
        ),
    )(inputs, kernel, w_in, w_gate, w_out, factor_a, factor_b, cotangent)
    out, gin, gker, gwi, gwg, gwo, gfa, gfb = outs
    shape = (NB, 128, 128)
    return (
        out,
        gin,
        gker,
        gwi.reshape(shape),
        gwg.reshape(shape),
        gwo.reshape(shape),
        gfa,
        gfb,
    )


def solution(mesh):
    return jax.shard_map(
        body,
        mesh=mesh,
        in_specs=(
            P("tm", "tensor"),
            P("tm", "tensor"),
            P("tensor", None, None),
            P("tensor", None, None),
            P("tensor", None, None),
            P(),
            P(),
            P("tm", "tensor"),
        ),
        out_specs=(
            P("tm", "tensor"),
            P("tm", "tensor"),
            P("tm", "tensor"),
            P("tensor", None, None),
            P("tensor", None, None),
            P("tensor", None, None),
            P("tm", None),
            P("tm", None),
        ),
        check_vma=False,
    )
```

time: 1060 us -> 129 us (0.12)
  waiting for transfers between devices: 831 us -> 0 us
  Pallas kernels: 0 us -> 119 us
  blocking collectives: 77.7 us -> 0 us
  local copies, waits for them, and re-layouts: 72.9 us -> 9.2 us
  matrix products: 32.4 us -> 0 us
  between operations: 14.9 us -> 0.67 us
  starting transfers between devices: 13.3 us -> 0 us
  other arithmetic: 12.3 us -> 0 us
    psum x1 -> x0, waiting for transfers between devices: 523 us -> none  [body(): lax.psum((mixer_terms[0], mixer_terms[1], mixer_terms[2]), 'tm')]
    reduce_scatter x1 -> x0, waiting for transfers between devices: 289 us -> none  [body(): lax.psum_scatter(factor_terms[0], 'tm', scatter_dimension=0, tiled=True)]
    pallas_call x0 -> x1, Pallas kernels: none -> 119 us  [body(): pl.pallas_call(kernel_body, name='monarch', out_shape=(big, big, big, til...]
    all_to_all x2 -> x0, blocking collectives: 61.5 us -> none  [to_columns(): return lax.all_to_all(values, 'tm', split_axis=1, concat_axis=0, tiled=True)]
    convert_element_type x14 -> x0, local copies, waits for them, and re-layouts: 49.7 us -> none  [the longest x3 12.6 us: body(): second32 = second.astype(jnp.float32)]
    dot_general x15 -> x0, matrix products: 32.4 us -> none  [the longest x1 6.01 us: body(): jnp.einsum('ijc,jk->ikc', mixed3, factor_a, preferred_element_type=jnp.fl...]
    all_to_all x2 -> x0, waiting for transfers between devices: 18.9 us -> none  [to_rows(): return lax.all_to_all(values, 'tm', split_axis=0, concat_axis=1, tiled=True)]
    psum x1 -> x0, blocking collectives: 16.2 us -> none  [body(): factor_terms = lax.psum((factor_terms[0], factor_terms[1]), 'tensor')]
  transfers between devices with their start and end apart: 4 -> 0, of which waited for: 4 -> 0; matrix products, arithmetic and copies ran while one was open for 4% -> 0% of each run, Pallas kernels for 0% -> 0%
where the time goes in v1:
time: 129 us
  Pallas kernels  119 us (92%)
  local copies, waits for them, and re-layouts  9.2 us (7%)
    pallas_call x1, Pallas kernels, body(): pl.pallas_call(kernel_body, name='monarch', out_shape=(big, big, big, til...  119 us
    unnamed x22, local copies, waits for them, and re-layouts  9.2 us

profile of v1, /device:TPU:1, one launch (start us, length us, event | category | flops | bytes accessed | tf_op | source)
XLA Modules:
  0.0 129.2 jit_solution(5509070013063323952)
XLA Ops:
  0.6 119.3 %monarch.1 = (bf16[2048,384]{1,0:T(8,128)(2,1)}, bf16[2048,384]{1,0:T(8,128)(2,1)}, bf16[2048,384]{1,0:T(8,128)(2,1)}, f32[48,8,128]{2,1,0:T(8,128)}, f32[48,8,1...) custom-call(bf16[2048,384]{1,0:T(8,128)(2,1)} %in_h.1, bf16[2048,384]{1,0:T(8,128)(2,1)} %ker_h.1, ...), custom_call_target="tpu_custom_call" | custom-call | tf_op jit(solution)/shard_map/monarch/pallas_call | solution.py:403
  120.0 0.0 copy-start.1
  120.0 2.8 %copy.24 = bf16[2048,384]{1,0:T(8,128)(2,1)} copy(bf16[2048,384]{1,0:T(8,128)(2,1)} %get-tuple-element.32) | data formatting | bytes 3145728
  122.8 0.0 copy-done.1
  122.8 0.0 copy-start
  122.8 1.1 copy.25
  124.0 0.8 copy-done
  124.8 0.0 copy-start.4
  124.8 0.0 copy-start.3
  124.8 0.0 copy-start.2
  124.8 0.0 copy-start.5
  124.8 0.0 copy-start.6
  124.8 1.1 copy.26
  126.0 0.0 copy-done.4
  126.0 0.7 copy.27
  126.7 0.0 copy-done.3
  126.7 0.7 copy.28
  127.3 0.0 copy-done.2
  127.3 0.7 copy.29
  128.0 0.0 copy-done.5
  128.0 0.6 copy.30
  128.6 0.0 copy-done.6
  128.6 0.6 copy.31
Async XLA Ops:
  120.0 2.8 %copy-start.1 = (bf16[2048,384]{1,0:T(8,128)(2,1)S(1)}, bf16[2048,384]{1,0:T(8,128)(2,1)}, u32[]{:S(2)}) copy-start(bf16[2048,384]{1,0:T(8,128)(2,1)} %get-tuple-element.33) | copy-start | bytes 4718596
  122.8 2.0 %copy-start = (bf16[2048,384]{1,0:T(8,128)(2,1)S(1)}, bf16[2048,384]{1,0:T(8,128)(2,1)}, u32[]{:S(2)}) copy-start(bf16[2048,384]{1,0:T(8,128)(2,1)} %get-tuple-element.34) | copy-start | bytes 4718596
  124.8 1.2 copy-start.4
  124.8 1.8 %copy-start.3 = (f32[48,8,128]{2,1,0:T(8,128)S(1)}, f32[48,8,128]{2,1,0:T(8,128)}, u32[]{:S(2)}) copy-start(f32[48,8,128]{2,1,0:T(8,128)} %get-tuple-element.20) | copy-start | bytes 589828
  124.8 2.5 %copy-start.2 = (f32[48,8,128]{2,1,0:T(8,128)S(1)}, f32[48,8,128]{2,1,0:T(8,128)}, u32[]{:S(2)}) copy-start(f32[48,8,128]{2,1,0:T(8,128)} %get-tuple-element.21) | copy-start | bytes 589828
  124.8 3.2 %copy-start.5 = (f32[8,512]{1,0:T(8,128)S(1)}, f32[8,512]{1,0:T(8,128)}, u32[]{:S(2)}) copy-start(f32[8,512]{1,0:T(8,128)} %get-tuple-element.38) | copy-start | bytes 49156
  124.8 3.8 %copy-start.6 = (f32[4,256]{1,0:T(4,128)S(1)}, f32[4,256]{1,0:T(4,128)}, u32[]{:S(2)}) copy-start(f32[4,256]{1,0:T(4,128)} %get-tuple-element.39) | copy-start | bytes 12292

commit v2 on v1

--- a/solution.py
+++ b/solution.py
@@ -20,6 +20,7 @@
 LOC = 4
 KD = 8
 NB = 3
+OWN = 48
 DC = 8
 CR = DC * KD
 
@@ -78,9 +79,9 @@
     fa,
     fb,
     cot_h,
-    out_h,
-    gin_h,
-    gker_h,
+    out_v,
+    gin_v,
+    gker_v,
     gw_in,
     gw_gate,
     gw_out,
@@ -112,13 +113,11 @@
     gm_v,
     gated_v,
     ggate_v,
-    out_v,
-    gin_v,
-    gker_v,
     fb_acc,
     fa_acc,
     r1s,
     r1r,
+    rp,
     r2s,
     r2r,
     tr,
@@ -126,24 +125,30 @@
     ag1,
     ag2,
     ld_sem,
-    st_sem,
     snd,
     rcv,
 ):
     me = lax.axis_index("tm")
     te = lax.axis_index("tensor")
-    core = lax.rem(me, 2)
-    my = lax.rem(me // 2, 4)
-    mx = lax.rem(me // 8, 4)
-    mz = me // 32
-
-    def peer(p):
-        o = lax.rem((p - 1) * 37, 63) + 1
-        dc = lax.rem(core + lax.rem(o, 2), 2)
-        dy = lax.rem(my + lax.rem(o // 2, 4), 4)
-        dx = lax.rem(mx + lax.rem(o // 8, 4), 4)
-        dz = lax.rem(mz + o // 32, 2)
-        return ((dz * 4 + dx) * 4 + dy) * 2 + dc
+    core = me & 1
+    my = (me >> 1) & 3
+    mx = (me >> 3) & 3
+    mz = me >> 5
+    chip = me >> 1
+
+    def each_peer(fn, cores=(0, 1)):
+        for dz, dc in ((0, 1), (1, 0), (1, 1)):
+            if dc in cores:
+                fn((((mz ^ dz) * 4 + mx) * 4 + my) * 2 + (core ^ dc))
+
+        @pl.loop(1, 16)
+        def _(p):
+            q = (p * 5) & 15
+            x = (mx + (q >> 2)) & 3
+            y = (my + q) & 3
+            for dz in (0, 1):
+                for dc in cores:
+                    fn((((mz ^ dz) * 4 + x) * 4 + y) * 2 + (core ^ dc))
 
     loads = [
         pltpu.make_async_copy(cot_h, cot_v, ld_sem.at[0]),
@@ -155,9 +160,9 @@
 
     barrier = pltpu.get_barrier_semaphore()
 
-    @pl.loop(1, TM)
-    def _(p):
-        pl.semaphore_signal(barrier, inc=1, device_id=(peer(p), te), device_id_type=MESH)
+    each_peer(
+        lambda d: pl.semaphore_signal(barrier, inc=1, device_id=(d, te), device_id_type=MESH)
+    )
 
     for q in range(1, TE):
         pl.semaphore_signal(
@@ -175,10 +180,7 @@
         )
 
     def send_all(slot_of, dst, ph):
-        @pl.loop(1, TM)
-        def _(p):
-            d = peer(p)
-            copy_to(slot_of(d), dst.at[me], ph, (d, te)).start()
+        each_peer(lambda d: copy_to(slot_of(d), dst.at[me], ph, (d, te)).start())
 
     def wait_slots(ref, sem, slots=TM - 1):
         part = ref.at[pl.ds(0, slots)]
@@ -293,13 +295,6 @@
             put_four(gf_v, c, n, gf)
             put_four(gker_v, c, n, gk)
 
-    stores = [
-        pltpu.make_async_copy(gker_v, gker_h, st_sem.at[0]),
-        pltpu.make_async_copy(out_v, out_h, st_sem.at[1]),
-        pltpu.make_async_copy(gin_v, gin_h, st_sem.at[2]),
-    ]
-    stores[0].start()
-
     fa_acc[...] = jnp.zeros_like(fa_acc)
 
     @pl.loop(0, LOC)
@@ -314,8 +309,18 @@
             8, 2, 8, 128
         )
     r1s[24:32, :, :, 640:768] = jnp.zeros((8, 2, 8, 128), F32)
-    send_all(lambda d: r1s.at[d // 2, lax.rem(d, 2)], r1r, 4)
-    r1r[me] = r1s[me // 2, core]
+    half = copy_to(r1s.at[:, 1 - core], rp, 10, (me ^ 1, te))
+    half.start()
+    half.wait_recv()
+
+    @pl.loop(0, TM // 2)
+    def _(g):
+        rp[g] += r1s[g, core]
+
+    each_peer(
+        lambda d: copy_to(rp.at[d >> 1], r1r.at[chip], 4, (d, te)).start(), cores=(0,)
+    )
+    r1r[chip] = rp[chip]
 
     wait_slots(rr_f, rcv.at[3])
 
@@ -331,9 +336,17 @@
     for n in range(NB):
         r2s[n * 16 : (n + 1) * 16, 0] = nn(in_t[n], ggate_v[:, lanes(n)]).reshape(16, 8, 128)
         r2s[n * 16 : (n + 1) * 16, 1] = nn(cot_t[n], gated_v[:, lanes(n)]).T.reshape(16, 8, 128)
-    r2s[48:64] = jnp.zeros((16, 2, 8, 128), F32)
-    send_all(lambda d: r2s.at[d], r2r, 7)
-    r2r[me] = r2s[me]
+
+    def send_r2(d):
+        @pl.when(d < OWN)
+        def _():
+            copy_to(r2s.at[d], r2r.at[me], 7, (d, te)).start()
+
+    each_peer(send_r2)
+
+    @pl.when(me < OWN)
+    def _():
+        r2r[me] = r2s[me]
 
     @pl.loop(0, ROWS // 256)
     def _(c):
@@ -344,22 +357,23 @@
                 nt(gm_v[rows, lanes(n)], w_in[n]) + nt(ggate_v[rows, lanes(n)], w_gate[n])
             ).astype(BF16)
 
-    stores[1].start()
-    stores[2].start()
+    def four_slots(q):
+        return (r1r[q * 4] + r1r[q * 4 + 1]) + (r1r[q * 4 + 2] + r1r[q * 4 + 3])
 
     token_scale = 1.0 / math.sqrt(N1 * N2)
-    wait_slots(r1r, rcv.at[4])
-    sum1 = lax.fori_loop(1, TM, lambda q, acc: acc + r1r[q], r1r[0])
+    wait_slots(r1r, rcv.at[4], TM // 2 - 1)
+    sum1 = lax.fori_loop(0, TM // 8, lambda q, acc: acc + four_slots(q), jnp.zeros((8, 768), F32))
     tr[te] = sum1[:, 0:640]
     for q in range(1, TE):
         copy_to(tr.at[te], tr.at[te], 5, (me, lax.rem(te + q, TE))).start()
-    ag1[me] = sum1[:, 640:768] * token_scale
-    send_all(lambda d: ag1.at[me], ag1, 8)
-
-    wait_slots(r2r, rcv.at[7])
-    sum2 = lax.fori_loop(1, TM, lambda q, acc: acc + r2r[q], r2r[0])
-    ag2[me] = sum2 * token_scale
-    send_all(lambda d: ag2.at[me], ag2, 9)
+
+    @pl.when(me < OWN)
+    def _():
+        ag1[me] = sum1[:, 640:768] * token_scale
+        send_all(lambda d: ag1.at[me], ag1, 8)
+        wait_slots(r2r, rcv.at[7])
+        ag2[me] = jnp.sum(r2r[...], axis=0) * token_scale
+        send_all(lambda d: ag2.at[me], ag2, 9)
 
     wait_slots(tr, rcv.at[5], TE - 1)
     total = tr[0] + tr[1] + tr[2] + tr[3]
@@ -371,21 +385,49 @@
     for h in range(2):
         gfb[:, lanes(h)] = jnp.where(core == 0, pr[h, 0:4, :], pr[h, 4:8, :])
 
-    wait_slots(ag1, rcv.at[8])
-    gw_in[...] = ag1[0:48]
-    wait_slots(ag2, rcv.at[9])
-    gw_gate[...] = ag2[0:48, 0]
-    gw_out[...] = ag2[0:48, 1]
+    def others(fn):
+        @pl.when(me < OWN)
+        def _():
+            fn(OWN - 1)
+
+        @pl.when(me >= OWN)
+        def _():
+            fn(OWN)
+
+    others(lambda k: wait_slots(ag1, rcv.at[8], k))
+    gw_in[...] = ag1[...]
+    others(lambda k: wait_slots(ag2, rcv.at[9], k))
+    gw_gate[...] = ag2[:, 0]
+    gw_out[...] = ag2[:, 1]
 
     wait_slots(rc_g, snd.at[0])
     wait_slots(rc_f, snd.at[1])
     wait_slots(rr_g, snd.at[2])
     wait_slots(rr_f, snd.at[3])
-    wait_slots(r1r, snd.at[4])
+    wait_slots(r1r, snd.at[4], TM // 2 - 1)
     wait_slots(tr, snd.at[5], TE - 1)
-    wait_slots(r2r, snd.at[7])
-    wait_slots(ag1, snd.at[8])
-    wait_slots(ag2, snd.at[9])
+    others(lambda k: wait_slots(r2r, snd.at[7], k))
+
+    @pl.when(me < OWN)
+    def _():
+        for part in (ag1.at[pl.ds(0, 48)], ag1.at[pl.ds(0, 15)]):
+            pltpu.make_async_copy(part, part, snd.at[8]).wait()
+        wait_slots(r2r, snd.at[9])
+
+    half.wait_send()
+
+
+def finish_body(*refs):
+    srcs, dsts, sem = refs[:8], refs[8:16], refs[16]
+    stores = []
+    for src, dst in zip(srcs, dsts, strict=True):
+        cuts = 4 if src.shape[0] == ROWS else 1
+        step = src.shape[0] // cuts
+        for j in range(cuts):
+            rows = pl.ds(j * step, step)
+            stores.append(pltpu.make_async_copy(src.at[rows], dst.at[rows], sem.at[len(stores)]))
+    for cp in stores:
+        cp.start()
     for cp in stores:
         cp.wait()
 
@@ -393,28 +435,27 @@
 def body(inputs, kernel, w_in, w_gate, w_out, factor_a, factor_b, cotangent):
     any_spec = pl.BlockSpec(memory_space=pl.ANY)
     vm = pl.BlockSpec(memory_space=pltpu.VMEM)
-    big = jax.ShapeDtypeStruct((ROWS, CH), BF16)
     wide = pltpu.VMEM((ROWS, CH), F32)
     act = pltpu.VMEM((ROWS, CH), BF16)
     turned = pltpu.VMEM((NB, 128, ROWS), BF16)
     slots = pltpu.VMEM((TM, LOC * KD, CH), BF16)
     cols = pltpu.VMEM((KD, N1, CH), BF16)
-    tile = jax.ShapeDtypeStruct((48, 8, 128), F32)
+    tile = pltpu.VMEM((OWN, 8, 128), F32)
     outs = pl.pallas_call(
         kernel_body,
         name="monarch",
         out_shape=(
-            big,
-            big,
-            big,
+            act,
+            act,
+            act,
             tile,
             tile,
             tile,
-            jax.ShapeDtypeStruct((8, N2), F32),
-            jax.ShapeDtypeStruct((4, N1), F32),
+            pltpu.VMEM((8, N2), F32),
+            pltpu.VMEM((4, N1), F32),
         ),
         in_specs=[any_spec, any_spec, vm, vm, vm, vm, vm, any_spec],
-        out_specs=(any_spec, any_spec, any_spec, vm, vm, vm, vm, vm),
+        out_specs=(vm,) * 8,
         scratch_shapes=[
             act,
             act,
@@ -442,28 +483,34 @@
             act,
             act,
             act,
-            act,
-            act,
-            act,
             pltpu.VMEM((N1, N1), F32),
             pltpu.VMEM((N2, N2), F32),
             pltpu.VMEM((TM // 2, 2, 8, 768), F32),
-            pltpu.VMEM((TM, 8, 768), F32),
-            pltpu.VMEM((TM, 2, 8, 128), F32),
+            pltpu.VMEM((TM // 2, 8, 768), F32),
+            pltpu.VMEM((TM // 2, 8, 768), F32),
+            pltpu.VMEM((OWN, 2, 8, 128), F32),
             pltpu.VMEM((TM, 2, 8, 128), F32),
             pltpu.VMEM((TE, 8, 640), F32),
             pltpu.VMEM((2, 8, 128), F32),
-            pltpu.VMEM((TM, 8, 128), F32),
-            pltpu.VMEM((TM, 2, 8, 128), F32),
+            pltpu.VMEM((OWN, 8, 128), F32),
+            pltpu.VMEM((OWN, 2, 8, 128), F32),
             pltpu.SemaphoreType.DMA((3,)),
-            pltpu.SemaphoreType.DMA((3,)),
-            pltpu.SemaphoreType.DMA((10,)),
-            pltpu.SemaphoreType.DMA((10,)),
+            pltpu.SemaphoreType.DMA((11,)),
+            pltpu.SemaphoreType.DMA((11,)),
         ],
         compiler_params=pltpu.CompilerParams(
-            collective_id=0, has_side_effects=True, vmem_limit_bytes=67043328
+            collective_id=0, has_side_effects=True, vmem_limit_bytes=57 << 20
         ),
     )(inputs, kernel, w_in, w_gate, w_out, factor_a, factor_b, cotangent)
+    outs = pl.pallas_call(
+        finish_body,
+        name="finish",
+        out_shape=tuple(jax.ShapeDtypeStruct(o.shape, o.dtype) for o in outs),
+        in_specs=[vm] * len(outs),
+        out_specs=(any_spec,) * len(outs),
+        scratch_shapes=[pltpu.SemaphoreType.DMA((17,))],
+        compiler_params=pltpu.CompilerParams(vmem_limit_bytes=8 << 20),
+    )(*outs)
     out, gin, gker, gwi, gwg, gwo, gfa, gfb = outs
     shape = (NB, 128, 128)
     return (

time: 129 us -> 111 us (0.86)
  local copies, waits for them, and re-layouts: 9.2 us -> 0 us
  Pallas kernels: 119 us -> 110 us
    pallas_call x1 -> x2, Pallas kernels: 119 us -> 110 us  [the longest x1 108 us: body(): pl.pallas_call(kernel_body, name='monarch', out_shape=(act, act, act, til...]
    unnamed x22 -> x0, local copies, waits for them, and re-layouts: 9.2 us -> none
where the time goes in v2:
time: 111 us
  Pallas kernels  110 us (99%)
    pallas_call x1, Pallas kernels, body(): pl.pallas_call(kernel_body, name='monarch', out_shape=(act, act, act, til...  108 us
    pallas_call x1, Pallas kernels, body(): pl.pallas_call(finish_body, name='finish', out_shape=tuple((jax.ShapeDtyp...  2.49 us

profile of v2, /device:TPU:1, one launch (start us, length us, event | category | flops | bytes accessed | tf_op | source)
XLA Modules:
  0.0 110.7 jit_solution(11546175978454207948)
XLA Ops:
  0.6 107.5 %monarch.1 = (bf16[2048,384]{1,0:T(8,128)(2,1)S(1)}, bf16[2048,384]{1,0:T(8,128)(2,1)S(1)}, bf16[2048,384]{1,0:T(8,128)(2,1)S(1)}, f32[48,8,128]{2,1,0:T(8,128)S...) custom-call(bf16[2048,384]{1,0:T(8,128)(2,1)} %in_h.1, ...), custom_call_target="tpu_custom_call" | custom-call | tf_op jit(solution)/shard_map/monarch/pallas_call | solution.py:444
  108.2 2.5 %finish.1 = (bf16[2048,384]{1,0:T(8,128)(2,1)}, bf16[2048,384]{1,0:T(8,128)(2,1)}, bf16[2048,384]{1,0:T(8,128)(2,1)}, f32[48,8,128]{2,1,0:T(8,128)}, f32[48,8,12...) custom-call(bf16[2048,384]{1,0:T(8,128)(2,1)S(1)} %get-tuple-element.24.refs_0_, ...), custom_call_target="tpu_custom_call" | custom-call | tf_op jit(solution)/shard_map/finish/pallas_call | solution.py:505

commit v3 on v2

--- a/solution.py
+++ b/solution.py
@@ -73,11 +73,11 @@
 def kernel_body(
     in_h,
     ker_h,
-    w_in,
-    w_gate,
-    w_out,
-    fa,
-    fb,
+    wi_h,
+    wg_h,
+    wo_h,
+    fa_h,
+    fb_h,
     cot_h,
     out_v,
     gin_v,
@@ -90,6 +90,11 @@
     in_v,
     ker_v,
     cot_v,
+    w_in,
+    w_gate,
+    w_out,
+    fa,
+    fb,
     in_t,
     cot_t,
     a_t,
@@ -117,6 +122,7 @@
     fa_acc,
     r1s,
     r1r,
+    r1b,
     rp,
     r2s,
     r2r,
@@ -151,9 +157,19 @@
                     fn((((mz ^ dz) * 4 + x) * 4 + y) * 2 + (core ^ dc))
 
     loads = [
-        pltpu.make_async_copy(cot_h, cot_v, ld_sem.at[0]),
-        pltpu.make_async_copy(in_h, in_v, ld_sem.at[1]),
-        pltpu.make_async_copy(ker_h, ker_v, ld_sem.at[2]),
+        pltpu.make_async_copy(src, dst, ld_sem.at[j])
+        for j, (src, dst) in enumerate(
+            (
+                (wg_h, w_gate),
+                (wo_h, w_out),
+                (cot_h, cot_v),
+                (in_h, in_v),
+                (wi_h, w_in),
+                (fa_h, fa),
+                (ker_h, ker_v),
+                (fb_h, fb),
+            )
+        )
     ]
     for cp in loads:
         cp.start()
@@ -186,8 +202,8 @@
         part = ref.at[pl.ds(0, slots)]
         pltpu.make_async_copy(part, part, sem).wait()
 
-    loads[0].wait()
-    loads[1].wait()
+    for cp in loads[:4]:
+        cp.wait()
 
     @pl.loop(0, N2 // CR)
     def _(c):
@@ -203,6 +219,8 @@
     pl.semaphore_wait(barrier, TM - 1 + TE - 1)
     send_all(lambda d: so_g.at[d], rc_g, 0)
 
+    loads[4].wait()
+    loads[5].wait()
     for s in range(4):
         a_t[:, lanes(s)] = fa[lanes(s), :].T
 
@@ -213,7 +231,7 @@
             mx_v[rows, lanes(n)] = nn(in_v[rows, lanes(n)], w_in[n]).astype(BF16)
         first_v[rows, :] = nn(a_t[...], mx_v[rows, :])
 
-    loads[2].wait()
+    loads[6].wait()
 
     @pl.loop(0, N2 // CR)
     def _(c):
@@ -227,6 +245,7 @@
     rc_g[me] = so_g[me]
     rc_f[me] = so_f[me]
 
+    loads[7].wait()
     b_t[...] = fb[...].T
 
     @pl.loop(0, ROWS // 256)
@@ -247,7 +266,7 @@
             for n in range(NB):
                 x[k, :, lanes(n)] = xs[n, pl.ds(k, N1, stride=KD), :].astype(BF16)
 
-    def product(lhs, x, sr):
+    def product(lhs, x, slab):
         for k in range(KD):
             y = nn(lhs[...], x[k])
             for n in range(NB):
@@ -257,21 +276,21 @@
         def _(c):
             rows = pl.ds(pl.multiple_of(c * 256, 256), 256)
             for n in range(NB):
-                sr[pl.ds(c * 8, 8), :, lanes(n)] = (
-                    xs[n, rows, :].astype(BF16).reshape(8, LOC * KD, 128)
-                )
+                slab(c, n)[...] = xs[n, rows, :].astype(BF16).reshape(8, LOC * KD, 128)
 
     wait_slots(rc_g, rcv.at[0])
     columns(rc_g, x_g)
-    product(fb, x_g, sr_g)
+    product(fb, x_g, lambda c, n: sr_g.at[pl.ds(c * 8, 8), :, lanes(n)])
     send_all(lambda d: sr_g.at[d], rr_g, 2)
     rr_g[me] = sr_g[me]
 
     wait_slots(rc_f, rcv.at[1])
     columns(rc_f, x_f)
-    product(b_t, x_f, sr_f)
-    send_all(lambda d: sr_f.at[d], rr_f, 3)
-    rr_f[me] = sr_f[me]
+    product(b_t, x_f, lambda c, n: sr_f.at[n, pl.ds(c * 8, 8)])
+    for n in range(NB):
+        send_all(lambda d, n=n: sr_f.at[n, d], rr_f.at[n], 3 + n)
+    for n in range(NB):
+        rr_f[n, me] = sr_f[n, me]
 
     fb_acc[...] = nt(x_f[0], x_g[0])
 
@@ -309,44 +328,49 @@
             8, 2, 8, 128
         )
     r1s[24:32, :, :, 640:768] = jnp.zeros((8, 2, 8, 128), F32)
-    half = copy_to(r1s.at[:, 1 - core], rp, 10, (me ^ 1, te))
+    half = copy_to(r1s.at[:, 1 - core], rp, 9, (me ^ 1, te))
     half.start()
-    half.wait_recv()
-
-    @pl.loop(0, TM // 2)
-    def _(g):
-        rp[g] += r1s[g, core]
-
-    each_peer(
-        lambda d: copy_to(rp.at[d >> 1], r1r.at[chip], 4, (d, te)).start(), cores=(0,)
-    )
-    r1r[chip] = rp[chip]
-
-    wait_slots(rr_f, rcv.at[3])
-
-    @pl.loop(0, N2 // CR)
-    def _(c):
-        for n in range(NB):
+
+    def forward_tail(n):
+        wait_slots(rr_f.at[n], rcv.at[3 + n])
+
+        @pl.loop(0, N2 // CR)
+        def _(c):
             sec = by_block(
-                rr_f[pl.ds(c * DC, DC), :, lanes(n)].reshape(LOC * CR, 128).astype(F32)
+                rr_f[n, pl.ds(c * DC, DC)].reshape(LOC * CR, 128).astype(F32)
             )
             put_four(gated_v, c, n, (sec * four(gate_v, c, n)).astype(BF16))
             put_four(ggate_v, c, n, (sec * four(gg_v, c, n)).astype(BF16))
 
-    for n in range(NB):
-        r2s[n * 16 : (n + 1) * 16, 0] = nn(in_t[n], ggate_v[:, lanes(n)]).reshape(16, 8, 128)
-        r2s[n * 16 : (n + 1) * 16, 1] = nn(cot_t[n], gated_v[:, lanes(n)]).T.reshape(16, 8, 128)
-
-    def send_r2(d):
-        @pl.when(d < OWN)
+        r2s[n, 0:16] = nn(in_t[n], ggate_v[:, lanes(n)]).reshape(16, 8, 128)
+        r2s[n, 16:32] = nn(cot_t[n], gated_v[:, lanes(n)]).T.reshape(16, 8, 128)
+        own = n % 2
+
+        def send(d):
+            @pl.when((d & 1) == own)
+            def _():
+                copy_to(r2s.at[n, d >> 1], r2r.at[n, me], 11 + n, (d, te)).start()
+
+        each_peer(send)
+
+        @pl.when(core == own)
         def _():
-            copy_to(r2s.at[d], r2r.at[me], 7, (d, te)).start()
-
-    each_peer(send_r2)
-
-    @pl.when(me < OWN)
-    def _():
-        r2r[me] = r2s[me]
+            r2r[n, me] = r2s[n, chip]
+
+    forward_tail(0)
+    half.wait_recv()
+
+    @pl.loop(0, TM // 2)
+    def _(g):
+        both = rp[g] + r1s[g, core]
+        r1b[g] = jnp.concatenate([both[:, 0:CH], both[:, CH:]], axis=0).astype(BF16)
+
+    each_peer(
+        lambda d: copy_to(r1b.at[d >> 1], r1r.at[chip], 6, (d, te)).start(), cores=(0,)
+    )
+    r1r[chip] = r1b[chip]
+    forward_tail(1)
+    forward_tail(2)
 
     @pl.loop(0, ROWS // 256)
     def _(c):
@@ -358,63 +382,102 @@
             ).astype(BF16)
 
     def four_slots(q):
-        return (r1r[q * 4] + r1r[q * 4 + 1]) + (r1r[q * 4 + 2] + r1r[q * 4 + 3])
+        a, b, c, d = (r1r[q * 4 + j].astype(F32) for j in range(4))
+        return (a + b) + (c + d)
 
     token_scale = 1.0 / math.sqrt(N1 * N2)
-    wait_slots(r1r, rcv.at[4], TM // 2 - 1)
-    sum1 = lax.fori_loop(0, TM // 8, lambda q, acc: acc + four_slots(q), jnp.zeros((8, 768), F32))
-    tr[te] = sum1[:, 0:640]
+    wait_slots(r1r, rcv.at[6], TM // 2 - 1)
+    sum1 = lax.fori_loop(0, TM // 8, lambda q, acc: acc + four_slots(q), jnp.zeros((16, CH), F32))
+    tr[te, :, 0:CH] = sum1[0:8]
+    tr[te, :, CH:640] = sum1[8:16, 0:256]
     for q in range(1, TE):
-        copy_to(tr.at[te], tr.at[te], 5, (me, lax.rem(te + q, TE))).start()
+        copy_to(tr.at[te], tr.at[te], 7, (me, lax.rem(te + q, TE))).start()
+
+    def to_chips(piece, ph):
+        each_peer(lambda d: copy_to(piece, piece, ph, (d, te)).start(), cores=(0,))
 
     @pl.when(me < OWN)
     def _():
-        ag1[me] = sum1[:, 640:768] * token_scale
-        send_all(lambda d: ag1.at[me], ag1, 8)
-        wait_slots(r2r, rcv.at[7])
-        ag2[me] = jnp.sum(r2r[...], axis=0) * token_scale
-        send_all(lambda d: ag2.at[me], ag2, 9)
-
-    wait_slots(tr, rcv.at[5], TE - 1)
+        ag1[chip, core] = sum1[8:16, 256:CH] * token_scale
+        to_chips(ag1.at[chip, core], 10)
+
+    for n in range(NB):
+
+        @pl.when(core == n % 2)
+        def _(n=n):
+            wait_slots(r2r.at[n], rcv.at[11 + n])
+            ag2[n, chip] = jnp.sum(r2r[n], axis=0) * token_scale
+            to_chips(ag2.at[n, chip], 14 + n)
+
+    wait_slots(tr, rcv.at[7], TE - 1)
     total = tr[0] + tr[1] + tr[2] + tr[3]
     gfa[...] = total[:, 0:512] * (1.0 / math.sqrt(N1 * D))
     pr[core] = total[:, 512:640] * (1.0 / math.sqrt(N2 * D))
-    pair = copy_to(pr.at[core], pr.at[core], 6, (me + 1 - 2 * core, te))
+    pair = copy_to(pr.at[core], pr.at[core], 8, (me ^ 1, te))
     pair.start()
     pair.wait()
     for h in range(2):
         gfb[:, lanes(h)] = jnp.where(core == 0, pr[h, 0:4, :], pr[h, 4:8, :])
 
-    def others(fn):
-        @pl.when(me < OWN)
+    def either(cond, then, other):
+        @pl.when(cond)
         def _():
-            fn(OWN - 1)
-
-        @pl.when(me >= OWN)
+            then()
+
+        @pl.when(jnp.logical_not(cond))
         def _():
-            fn(OWN)
-
-    others(lambda k: wait_slots(ag1, rcv.at[8], k))
-    gw_in[...] = ag1[...]
-    others(lambda k: wait_slots(ag2, rcv.at[9], k))
-    gw_gate[...] = ag2[:, 0]
-    gw_out[...] = ag2[:, 1]
+            other()
+
+    other = (me ^ 1, te)
+    either(
+        me < OWN,
+        lambda: wait_slots(ag2.at[0], rcv.at[10], OWN // 2 - 1),
+        lambda: wait_slots(ag2.at[0], rcv.at[10], OWN // 2),
+    )
+    pass1 = copy_to(ag1.at[:, core], ag1.at[:, core], 17, other)
+    pass1.start()
+    for n in range(NB):
+
+        @pl.when(core == n % 2)
+        def _(n=n):
+            wait_slots(ag2.at[n], rcv.at[14 + n], TM // 2 - 1)
+            copy_to(ag2.at[n], ag2.at[n], 18 + n, other).start()
+
+    pass1.wait_recv()
+    gw_in[...] = ag1[...].reshape(OWN, 8, 128)
+    for n in range(NB):
+
+        @pl.when(core != n % 2)
+        def _(n=n):
+            wait_slots(ag2.at[n], rcv.at[18 + n], TM // 2)
+
+        gw_gate[n * 16 : (n + 1) * 16] = ag2[n, 0:16]
+        gw_out[n * 16 : (n + 1) * 16] = ag2[n, 16:32]
 
     wait_slots(rc_g, snd.at[0])
     wait_slots(rc_f, snd.at[1])
     wait_slots(rr_g, snd.at[2])
-    wait_slots(rr_f, snd.at[3])
-    wait_slots(r1r, snd.at[4], TM // 2 - 1)
-    wait_slots(tr, snd.at[5], TE - 1)
-    others(lambda k: wait_slots(r2r, snd.at[7], k))
+    for n in range(NB):
+        wait_slots(rr_f.at[n], snd.at[3 + n])
+        either(
+            core == n % 2,
+            lambda: wait_slots(r2r.at[n], snd.at[11 + n], TM // 2 - 1),
+            lambda: wait_slots(r2r.at[n], snd.at[11 + n], TM // 2),
+        )
+
+        @pl.when(core == n % 2)
+        def _(n=n):
+            wait_slots(ag2.at[n], snd.at[14 + n], TM // 2 - 1)
+            wait_slots(ag2.at[n], snd.at[18 + n], TM // 2)
+
+    wait_slots(r1r, snd.at[6], TM // 2 - 1)
+    wait_slots(tr, snd.at[7], TE - 1)
+    half.wait_send()
+    pass1.wait_send()
 
     @pl.when(me < OWN)
     def _():
-        for part in (ag1.at[pl.ds(0, 48)], ag1.at[pl.ds(0, 15)]):
-            pltpu.make_async_copy(part, part, snd.at[8]).wait()
-        wait_slots(r2r, snd.at[9])
-
-    half.wait_send()
+        wait_slots(ag2.at[0], snd.at[10], TM // 2 - 1)
 
 
 def finish_body(*refs):
@@ -439,6 +502,8 @@
     act = pltpu.VMEM((ROWS, CH), BF16)
     turned = pltpu.VMEM((NB, 128, ROWS), BF16)
     slots = pltpu.VMEM((TM, LOC * KD, CH), BF16)
+    mixer = pltpu.VMEM((NB, 128, 128), BF16)
+    slots_n = pltpu.VMEM((NB, TM, LOC * KD, 128), BF16)
     cols = pltpu.VMEM((KD, N1, CH), BF16)
     tile = pltpu.VMEM((OWN, 8, 128), F32)
     outs = pl.pallas_call(
@@ -454,12 +519,17 @@
             pltpu.VMEM((8, N2), F32),
             pltpu.VMEM((4, N1), F32),
         ),
-        in_specs=[any_spec, any_spec, vm, vm, vm, vm, vm, any_spec],
+        in_specs=[any_spec] * 8,
         out_specs=(vm,) * 8,
         scratch_shapes=[
             act,
             act,
             act,
+            mixer,
+            mixer,
+            mixer,
+            pltpu.VMEM((N2, N2), BF16),
+            pltpu.VMEM((N1, N1), BF16),
             turned,
             turned,
             pltpu.VMEM((N2, N2), BF16),
@@ -476,9 +546,9 @@
             cols,
             cols,
             slots,
+            slots_n,
             slots,
-            slots,
-            slots,
+            slots_n,
             act,
             act,
             act,
@@ -486,17 +556,18 @@
             pltpu.VMEM((N1, N1), F32),
             pltpu.VMEM((N2, N2), F32),
             pltpu.VMEM((TM // 2, 2, 8, 768), F32),
+            pltpu.VMEM((TM // 2, 16, CH), BF16),
+            pltpu.VMEM((TM // 2, 16, CH), BF16),
             pltpu.VMEM((TM // 2, 8, 768), F32),
-            pltpu.VMEM((TM // 2, 8, 768), F32),
-            pltpu.VMEM((OWN, 2, 8, 128), F32),
-            pltpu.VMEM((TM, 2, 8, 128), F32),
+            pltpu.VMEM((NB, TM // 2, 8, 128), F32),
+            pltpu.VMEM((NB, TM, 8, 128), F32),
             pltpu.VMEM((TE, 8, 640), F32),
             pltpu.VMEM((2, 8, 128), F32),
-            pltpu.VMEM((OWN, 8, 128), F32),
-            pltpu.VMEM((OWN, 2, 8, 128), F32),
-            pltpu.SemaphoreType.DMA((3,)),
-            pltpu.SemaphoreType.DMA((11,)),
-            pltpu.SemaphoreType.DMA((11,)),
+            pltpu.VMEM((OWN // 2, 2, 8, 128), F32),
+            pltpu.VMEM((NB, TM // 2, 8, 128), F32),
+            pltpu.SemaphoreType.DMA((8,)),
+            pltpu.SemaphoreType.DMA((21,)),
+            pltpu.SemaphoreType.DMA((21,)),
         ],
         compiler_params=pltpu.CompilerParams(
             collective_id=0, has_side_effects=True, vmem_limit_bytes=57 << 20

time: 111 us -> 103 us (0.928)
  Pallas kernels: 110 us -> 102 us
    pallas_call x1, Pallas kernels: 108 us -> 99.7 us  [body(): pl.pallas_call(kernel_body, name='monarch', out_shape=(act, act, act, til...]
where the time goes in v3:
time: 103 us
  Pallas kernels  102 us (99%)
    pallas_call x1, Pallas kernels, body(): pl.pallas_call(kernel_body, name='monarch', out_shape=(act, act, act, til...  99.7 us
    pallas_call x1, Pallas kernels, body(): pl.pallas_call(finish_body, name='finish', out_shape=tuple((jax.ShapeDtyp...  2.49 us

profile of v3, /device:TPU:1, one launch (start us, length us, event | category | flops | bytes accessed | tf_op | source)
XLA Modules:
  0.0 102.9 jit_solution(14686804587031093577)
XLA Ops:
  0.6 99.7 %monarch.1 = (bf16[2048,384]{1,0:T(8,128)(2,1)S(1)}, bf16[2048,384]{1,0:T(8,128)(2,1)S(1)}, bf16[2048,384]{1,0:T(8,128)(2,1)S(1)}, f32[48,8,128]{2,1,0:T(8,128)S...) custom-call(bf16[2048,384]{1,0:T(8,128)(2,1)} %in_h.1, ...), custom_call_target="tpu_custom_call" | custom-call | tf_op jit(solution)/shard_map/monarch/pallas_call | solution.py:509
  100.4 2.5 %finish.1 = (bf16[2048,384]{1,0:T(8,128)(2,1)}, bf16[2048,384]{1,0:T(8,128)(2,1)}, bf16[2048,384]{1,0:T(8,128)(2,1)}, f32[48,8,128]{2,1,0:T(8,128)}, f32[48,8,12...) custom-call(bf16[2048,384]{1,0:T(8,128)(2,1)S(1)} %get-tuple-element.24.refs_0_, ...), custom_call_target="tpu_custom_call" | custom-call | tf_op jit(solution)/shard_map/finish/pallas_call | solution.py:576

commit v4 on v3

--- a/solution.py
+++ b/solution.py
@@ -143,17 +143,15 @@
     chip = me >> 1
 
     def each_peer(fn, cores=(0, 1)):
-        for dz, dc in ((0, 1), (1, 0), (1, 1)):
+        for dz, dc in ((1, 1), (0, 1), (1, 0), (0, 0)):
             if dc in cores:
-                fn((((mz ^ dz) * 4 + mx) * 4 + my) * 2 + (core ^ dc))
-
-        @pl.loop(1, 16)
-        def _(p):
-            q = (p * 5) & 15
-            x = (mx + (q >> 2)) & 3
-            y = (my + q) & 3
-            for dz in (0, 1):
-                for dc in cores:
+                here = dz + dc == 0
+
+                @pl.loop(int(here), 16, unroll=3 if here else 4)
+                def _(p, dz=dz, dc=dc):
+                    q = (p * 5) & 15
+                    x = (mx + (q >> 2)) & 3
+                    y = (my + q) & 3
                     fn((((mz ^ dz) * 4 + x) * 4 + y) * 2 + (core ^ dc))
 
     loads = [
@@ -342,8 +340,8 @@
             put_four(gated_v, c, n, (sec * four(gate_v, c, n)).astype(BF16))
             put_four(ggate_v, c, n, (sec * four(gg_v, c, n)).astype(BF16))
 
-        r2s[n, 0:16] = nn(in_t[n], ggate_v[:, lanes(n)]).reshape(16, 8, 128)
-        r2s[n, 16:32] = nn(cot_t[n], gated_v[:, lanes(n)]).T.reshape(16, 8, 128)
+        r2s[n, 0:16] = nn(in_t[n], ggate_v[:, lanes(n)]).reshape(16, 8, 128).astype(BF16)
+        r2s[n, 16:32] = nn(cot_t[n], gated_v[:, lanes(n)]).T.reshape(16, 8, 128).astype(BF16)
         own = n % 2
 
         def send(d):
@@ -406,8 +404,12 @@
         @pl.when(core == n % 2)
         def _(n=n):
             wait_slots(r2r.at[n], rcv.at[11 + n])
-            ag2[n, chip] = jnp.sum(r2r[n], axis=0) * token_scale
-            to_chips(ag2.at[n, chip], 14 + n)
+            ag2[n, chip] = jnp.sum(r2r[n].astype(F32), axis=0) * token_scale
+            if n < NB - 1:
+                to_chips(ag2.at[n, chip], 14 + n)
+            else:
+                piece = ag2.at[n, chip]
+                each_peer(lambda d: copy_to(piece, piece, 14 + n, (d, te)).start())
 
     wait_slots(tr, rcv.at[7], TE - 1)
     total = tr[0] + tr[1] + tr[2] + tr[3]
@@ -415,9 +417,6 @@
     pr[core] = total[:, 512:640] * (1.0 / math.sqrt(N2 * D))
     pair = copy_to(pr.at[core], pr.at[core], 8, (me ^ 1, te))
     pair.start()
-    pair.wait()
-    for h in range(2):
-        gfb[:, lanes(h)] = jnp.where(core == 0, pr[h, 0:4, :], pr[h, 4:8, :])
 
     def either(cond, then, other):
         @pl.when(cond)
@@ -436,21 +435,33 @@
     )
     pass1 = copy_to(ag1.at[:, core], ag1.at[:, core], 17, other)
     pass1.start()
-    for n in range(NB):
+    for n in range(NB - 1):
 
         @pl.when(core == n % 2)
         def _(n=n):
             wait_slots(ag2.at[n], rcv.at[14 + n], TM // 2 - 1)
             copy_to(ag2.at[n], ag2.at[n], 18 + n, other).start()
 
+    pair.wait()
+    for h in range(2):
+        gfb[:, lanes(h)] = jnp.where(core == 0, pr[h, 0:4, :], pr[h, 4:8, :])
+
     pass1.wait_recv()
     gw_in[...] = ag1[...].reshape(OWN, 8, 128)
     for n in range(NB):
 
-        @pl.when(core != n % 2)
-        def _(n=n):
-            wait_slots(ag2.at[n], rcv.at[18 + n], TM // 2)
-
+        if n < NB - 1:
+
+            @pl.when(core != n % 2)
+            def _(n=n):
+                wait_slots(ag2.at[n], rcv.at[18 + n], TM // 2)
+
+        else:
+            either(
+                core == n % 2,
+                lambda: wait_slots(ag2.at[n], rcv.at[14 + n], TM // 2 - 1),
+                lambda: wait_slots(ag2.at[n], rcv.at[14 + n], TM // 2),
+            )
         gw_gate[n * 16 : (n + 1) * 16] = ag2[n, 0:16]
         gw_out[n * 16 : (n + 1) * 16] = ag2[n, 16:32]
 
@@ -467,8 +478,12 @@
 
         @pl.when(core == n % 2)
         def _(n=n):
-            wait_slots(ag2.at[n], snd.at[14 + n], TM // 2 - 1)
-            wait_slots(ag2.at[n], snd.at[18 + n], TM // 2)
+            if n < NB - 1:
+                wait_slots(ag2.at[n], snd.at[14 + n], TM // 2 - 1)
+                wait_slots(ag2.at[n], snd.at[18 + n], TM // 2)
+            else:
+                wait_slots(ag2.at[n], snd.at[14 + n], TM // 2)
+                wait_slots(ag2.at[n], snd.at[14 + n], TM // 2 - 1)
 
     wait_slots(r1r, snd.at[6], TM // 2 - 1)
     wait_slots(tr, snd.at[7], TE - 1)
@@ -559,8 +574,8 @@
             pltpu.VMEM((TM // 2, 16, CH), BF16),
             pltpu.VMEM((TM // 2, 16, CH), BF16),
             pltpu.VMEM((TM // 2, 8, 768), F32),
-            pltpu.VMEM((NB, TM // 2, 8, 128), F32),
-            pltpu.VMEM((NB, TM, 8, 128), F32),
+            pltpu.VMEM((NB, TM // 2, 8, 128), BF16),
+            pltpu.VMEM((NB, TM, 8, 128), BF16),
             pltpu.VMEM((TE, 8, 640), F32),
             pltpu.VMEM((2, 8, 128), F32),
             pltpu.VMEM((OWN // 2, 2, 8, 128), F32),

time: 103 us -> 99.8 us (0.969)
  Pallas kernels: 102 us -> 99.1 us
    pallas_call x1, Pallas kernels: 99.7 us -> 96.6 us  [body(): pl.pallas_call(kernel_body, name='monarch', out_shape=(act, act, act, til...]
where the time goes in v4:
time: 99.8 us; the launch traced here: 99.7 us
  Pallas kernels  99.1 us (99%)
    pallas_call x1, Pallas kernels, body(): pl.pallas_call(kernel_body, name='monarch', out_shape=(act, act, act, til...  96.6 us
    pallas_call x1, Pallas kernels, body(): pl.pallas_call(finish_body, name='finish', out_shape=tuple((jax.ShapeDtyp...  2.49 us

profile of v4, /device:TPU:1, one launch (start us, length us, event | category | flops | bytes accessed | tf_op | source)
XLA Modules:
  0.0 99.7 jit_solution(3597637916783674766)
XLA Ops:
  0.6 96.6 %monarch.1 = (bf16[2048,384]{1,0:T(8,128)(2,1)S(1)}, bf16[2048,384]{1,0:T(8,128)(2,1)S(1)}, bf16[2048,384]{1,0:T(8,128)(2,1)S(1)}, f32[48,8,128]{2,1,0:T(8,128)S...) custom-call(bf16[2048,384]{1,0:T(8,128)(2,1)} %in_h.1, ...), custom_call_target="tpu_custom_call" | custom-call | tf_op jit(solution)/shard_map/monarch/pallas_call | solution.py:524
  97.2 2.5 %finish.1 = (bf16[2048,384]{1,0:T(8,128)(2,1)}, bf16[2048,384]{1,0:T(8,128)(2,1)}, bf16[2048,384]{1,0:T(8,128)(2,1)}, f32[48,8,128]{2,1,0:T(8,128)}, f32[48,8,12...) custom-call(bf16[2048,384]{1,0:T(8,128)(2,1)S(1)} %get-tuple-element.24.refs_0_, ...), custom_call_target="tpu_custom_call" | custom-call | tf_op jit(solution)/shard_map/finish/pallas_call | solution.py:591

commit v5 on v4

--- a/solution.py
+++ b/solution.py
@@ -411,40 +411,36 @@
                 piece = ag2.at[n, chip]
                 each_peer(lambda d: copy_to(piece, piece, 14 + n, (d, te)).start())
 
+    def either(cond, then, other):
+        @pl.when(cond)
+        def _():
+            then()
+
+        @pl.when(jnp.logical_not(cond))
+        def _():
+            other()
+
+    other = (me ^ 1, te)
+    either(
+        me < OWN,
+        lambda: wait_slots(ag2.at[0], rcv.at[10], OWN // 2 - 1),
+        lambda: wait_slots(ag2.at[0], rcv.at[10], OWN // 2),
+    )
+    pass1 = copy_to(ag1.at[:, core], ag1.at[:, core], 17, other)
+    pass1.start()
+    for n in range(NB - 1):
+
+        @pl.when(core == n % 2)
+        def _(n=n):
+            wait_slots(ag2.at[n], rcv.at[14 + n], TM // 2 - 1)
+            copy_to(ag2.at[n], ag2.at[n], 18 + n, other).start()
+
     wait_slots(tr, rcv.at[7], TE - 1)
     total = tr[0] + tr[1] + tr[2] + tr[3]
     gfa[...] = total[:, 0:512] * (1.0 / math.sqrt(N1 * D))
     pr[core] = total[:, 512:640] * (1.0 / math.sqrt(N2 * D))
     pair = copy_to(pr.at[core], pr.at[core], 8, (me ^ 1, te))
     pair.start()
-
-    def either(cond, then, other):
-        @pl.when(cond)
-        def _():
-            then()
-
-        @pl.when(jnp.logical_not(cond))
-        def _():
-            other()
-
-    other = (me ^ 1, te)
-    either(
-        me < OWN,
-        lambda: wait_slots(ag2.at[0], rcv.at[10], OWN // 2 - 1),
-        lambda: wait_slots(ag2.at[0], rcv.at[10], OWN // 2),
-    )
-    pass1 = copy_to(ag1.at[:, core], ag1.at[:, core], 17, other)
-    pass1.start()
-    for n in range(NB - 1):
-
-        @pl.when(core == n % 2)
-        def _(n=n):
-            wait_slots(ag2.at[n], rcv.at[14 + n], TM // 2 - 1)
-            copy_to(ag2.at[n], ag2.at[n], 18 + n, other).start()
-
-    pair.wait()
-    for h in range(2):
-        gfb[:, lanes(h)] = jnp.where(core == 0, pr[h, 0:4, :], pr[h, 4:8, :])
 
     pass1.wait_recv()
     gw_in[...] = ag1[...].reshape(OWN, 8, 128)
@@ -464,6 +460,10 @@
             )
         gw_gate[n * 16 : (n + 1) * 16] = ag2[n, 0:16]
         gw_out[n * 16 : (n + 1) * 16] = ag2[n, 16:32]
+
+    pair.wait()
+    for h in range(2):
+        gfb[:, lanes(h)] = jnp.where(core == 0, pr[h, 0:4, :], pr[h, 4:8, :])
 
     wait_slots(rc_g, snd.at[0])
     wait_slots(rc_f, snd.at[1])

time: 99.8 us -> 99.7 us (level)
  no operation moved by 1% of the time
where the time goes in v5:
time: 99.7 us; the launch traced here: 99.6 us
  Pallas kernels  99 us (99%)
    pallas_call x1, Pallas kernels, body(): pl.pallas_call(kernel_body, name='monarch', out_shape=(act, act, act, til...  96.5 us
    pallas_call x1, Pallas kernels, body(): pl.pallas_call(finish_body, name='finish', out_shape=tuple((jax.ShapeDtyp...  2.49 us

profile of v5, /device:TPU:1, one launch (start us, length us, event | category | flops | bytes accessed | tf_op | source)
XLA Modules:
  0.0 99.6 jit_solution(1771916313106377938)
XLA Ops:
  0.6 96.5 %monarch.1 = (bf16[2048,384]{1,0:T(8,128)(2,1)S(1)}, bf16[2048,384]{1,0:T(8,128)(2,1)S(1)}, bf16[2048,384]{1,0:T(8,128)(2,1)S(1)}, f32[48,8,128]{2,1,0:T(8,128)S...) custom-call(bf16[2048,384]{1,0:T(8,128)(2,1)} %in_h.1, ...), custom_call_target="tpu_custom_call" | custom-call | tf_op jit(solution)/shard_map/monarch/pallas_call | solution.py:524
  97.1 2.5 %finish.1 = (bf16[2048,384]{1,0:T(8,128)(2,1)}, bf16[2048,384]{1,0:T(8,128)(2,1)}, bf16[2048,384]{1,0:T(8,128)(2,1)}, f32[48,8,128]{2,1,0:T(8,128)}, f32[48,8,12...) custom-call(bf16[2048,384]{1,0:T(8,128)(2,1)S(1)} %get-tuple-element.24.refs_0_, ...), custom_call_target="tpu_custom_call" | custom-call | tf_op jit(solution)/shard_map/finish/pallas_call | solution.py:591

commit v6 on v4

--- a/solution.py
+++ b/solution.py
@@ -148,8 +148,8 @@
                 here = dz + dc == 0
 
                 @pl.loop(int(here), 16, unroll=3 if here else 4)
-                def _(p, dz=dz, dc=dc):
-                    q = (p * 5) & 15
+                def _(p, dz=dz, dc=dc, here=here):
+                    q = (p * 5 + (0 if here else 10)) & 15
                     x = (mx + (q >> 2)) & 3
                     y = (my + q) & 3
                     fn((((mz ^ dz) * 4 + x) * 4 + y) * 2 + (core ^ dc))

time: 99.8 us -> 99.8 us (level)
  no operation moved by 1% of the time
where the time goes in v6:
time: 99.8 us; the launch traced here: 99.7 us
  Pallas kernels  99.1 us (99%)
    pallas_call x1, Pallas kernels, body(): pl.pallas_call(kernel_body, name='monarch', out_shape=(act, act, act, til...  96.6 us
    pallas_call x1, Pallas kernels, body(): pl.pallas_call(finish_body, name='finish', out_shape=tuple((jax.ShapeDtyp...  2.49 us

profile of v6, /device:TPU:1, one launch (start us, length us, event | category | flops | bytes accessed | tf_op | source)
XLA Modules:
  0.0 99.7 jit_solution(14464845608586904894)
XLA Ops:
  0.6 96.6 %monarch.1 = (bf16[2048,384]{1,0:T(8,128)(2,1)S(1)}, bf16[2048,384]{1,0:T(8,128)(2,1)S(1)}, bf16[2048,384]{1,0:T(8,128)(2,1)S(1)}, f32[48,8,128]{2,1,0:T(8,128)S...) custom-call(bf16[2048,384]{1,0:T(8,128)(2,1)} %in_h.1, ...), custom_call_target="tpu_custom_call" | custom-call | tf_op jit(solution)/shard_map/monarch/pallas_call | solution.py:524
  97.2 2.5 %finish.1 = (bf16[2048,384]{1,0:T(8,128)(2,1)}, bf16[2048,384]{1,0:T(8,128)(2,1)}, bf16[2048,384]{1,0:T(8,128)(2,1)}, f32[48,8,128]{2,1,0:T(8,128)}, f32[48,8,12...) custom-call(bf16[2048,384]{1,0:T(8,128)(2,1)S(1)} %get-tuple-element.24.refs_0_, ...), custom_call_target="tpu_custom_call" | custom-call | tf_op jit(solution)/shard_map/finish/pallas_call | solution.py:591
